TPU v7x, 512 devices: a whole 4x8x8 slice. The times are simulated.
512 devices in a mesh: patch: 2 (over core), lat: 8 (over y), lon: 32 (over z, x).
Axes of the slice: x: 4, y: 8, z: 8, core: 2. Of those that a mesh axis runs over, the one named last changes fastest.
Arguments:
- velocity: float32 [2, 3, 128, 256, 128], P('patch', None, 'lat', 'lon'), may hold values from -6 to 6
- forcing: float32 [2, 3, 128, 256, 128], P('patch', None, 'lat', 'lon'), may hold values from -3 to 3
- viscosity: float32 [2, 128, 256, 128], P('patch', 'lat', 'lon'), may hold values from 1 to 10
- ghost_slots: int32 [2, 768], P('patch'), may hold values from 0 to 767, each once within a row
- corner_rows: int32 [2, 8, 96], P('patch', 'lat', 'lon'), may hold values from 0 to 15
- corner_cols: int32 [2, 8, 96], P('patch', 'lat', 'lon'), may hold values from 0 to 7
- corner_weights: float32 [2, 8, 4, 96], P('patch', 'lat', None, 'lon'), may hold values from 0 to 1, as said below
Outputs:
- new_velocity: float32 [2, 3, 128, 256, 128], P('patch', None, 'lat', 'lon')
- residual: float32 [2, 3, 128, 256, 128], P('patch', None, 'lat', 'lon')
Inputs may be any that keep to these rules, and one draw needn't show every extreme that they name: `ghost_slots`: each row names every slot of the other patch exactly once. `corner_rows`: the row below the corner is read too, from the next device or as zero beyond the patch. `corner_cols`: the column after the corner is read too, from the next device or as zero beyond the patch. `corner_weights`: the four weights of a slot are (1 - s)(1 - t), s(1 - t), (1 - s)t and st for some s and t in [0, 1).
All inputs are finite; a program needn't handle non-finite values.
Results may differ from a plain program's by a relative error of at most 0.0001.
Values sent between devices are 32-bit elements; how exact they have to be, the bound alone decides.
No kernel may reach another device: no remote copies, remote signals or barrier semaphores. Data moves between devices by JAX's collectives and lax.ppermute only.
A program may use at most 64 MiB of HBM per device.

v0:
```python
import jax
import jax.numpy as jnp
from jax import lax
from jax.sharding import PartitionSpec as P

SWEEPS = 2
COARSE = 8
RELAX = 0.8


def with_halo(shard, sides, width):
    for axis, dim in sides:
        devices, length = (lax.axis_size(axis), shard.shape[dim])
        up = [(i, (i + 1) % devices) for i in range(devices - 1)]
        down = [(j, i) for i, j in up]
        last = lax.slice_in_dim(shard, length - width, length, axis=dim)
        first = lax.slice_in_dim(shard, 0, width, axis=dim)
        before = lax.ppermute(last, axis, up)
        after = lax.ppermute(first, axis, down)
        shard = jnp.concatenate([before, shard, after], axis=dim)
    return shard


def swapped(value, axis, apart):
    mask = 2**apart
    pairs = [(source, source ^ mask) for source in range(lax.axis_size(axis))]
    return lax.ppermute(value, axis, pairs)


def face_terms(padded_visc, weight_scale):
    centre = padded_visc[1:-1, 1:-1, 1:-1]
    return (
        weight_scale * (centre + padded_visc[:-2, 1:-1, 1:-1]),
        weight_scale * (centre + padded_visc[2:, 1:-1, 1:-1]),
        weight_scale * (centre + padded_visc[1:-1, :-2, 1:-1]),
        weight_scale * (centre + padded_visc[1:-1, 2:, 1:-1]),
        weight_scale * (centre + padded_visc[1:-1, 1:-1, :-2]),
        weight_scale * (centre + padded_visc[1:-1, 1:-1, 2:]),
    )


def diagonal_of(face_coefs):
    return (
        face_coefs[0]
        + face_coefs[1]
        + face_coefs[2]
        + face_coefs[3]
        + face_coefs[4]
        + face_coefs[5]
    )


def neighbour_sum(padded, face_coefs):
    summed = face_coefs[0] * padded[:, :-2, 1:-1, 1:-1]
    summed = summed + face_coefs[1] * padded[:, 2:, 1:-1, 1:-1]
    summed = summed + face_coefs[2] * padded[:, 1:-1, :-2, 1:-1]
    summed = summed + face_coefs[3] * padded[:, 1:-1, 2:, 1:-1]
    summed = summed + face_coefs[4] * padded[:, 1:-1, 1:-1, :-2]
    summed = summed + face_coefs[5] * padded[:, 1:-1, 1:-1, 2:]
    return summed


def bilinear(weight_rows, corner_list):
    summed = weight_rows[0][None, :, None] * corner_list[0]
    summed = summed + weight_rows[1][None, :, None] * corner_list[1]
    summed = summed + weight_rows[2][None, :, None] * corner_list[2]
    summed = summed + weight_rows[3][None, :, None] * corner_list[3]
    return summed


def clamp_take(source_array, along_dim, offset, block_size, whole_size, margin):
    position = offset + jnp.arange(-margin, block_size + margin, dtype=jnp.int32)
    picked = jnp.clip(position, 0, whole_size - 1) - offset + margin
    return jnp.take(source_array, picked, axis=along_dim)


def per_device(velocity, forcing, viscosity, ghost_slots, corner_rows, corner_cols, corner_weights):
    start_field = velocity[0]
    force_block = forcing[0]
    viscous = viscosity[0]
    row_block, col_block, levels = viscous.shape
    lat_count = lax.axis_size("lat")
    lon_count = lax.axis_size("lon")
    lat_index = lax.axis_index("lat")
    lon_index = lax.axis_index("lon")
    lat_cells = row_block * lat_count
    lon_cells = col_block * lon_count
    row_offset = lat_index * row_block
    col_offset = lon_index * col_block
    ghost_count = ghost_slots.shape[1]
    order_row = ghost_slots[0]
    rim_width = 1
    visc_rim = with_halo(viscous, (("lat", 0), ("lon", 1)), 2)
    visc_ext = clamp_take(visc_rim, 0, row_offset, row_block, lat_cells, 2)
    visc_ext = clamp_take(visc_ext, 1, col_offset, col_block, lon_cells, 2)
    visc_ext = jnp.pad(visc_ext, ((0, 0), (0, 0), (2, 2)), mode="edge")
    loop_coefs = face_terms(visc_ext[:, :, 1:-1], 0.5)
    loop_diag = diagonal_of(loop_coefs)
    loop_rows = row_offset + jnp.arange(-1, row_block + 1, dtype=jnp.int32)
    loop_cols = col_offset + jnp.arange(-1, col_block + 1, dtype=jnp.int32)
    loop_parity = (
        loop_rows[:, None, None]
        + loop_cols[None, :, None]
        + jnp.arange(levels, dtype=jnp.int32)[None, None, :]
    ) % 2
    loop_inside = (
        ((loop_rows >= 0) & (loop_rows < lat_cells))[:, None]
        & ((loop_cols >= 0) & (loop_cols < lon_cells))[None, :]
    )[:, :, None]
    ext_rows = row_offset + jnp.arange(-rim_width, row_block + rim_width, dtype=jnp.int32)
    ext_cols = col_offset + jnp.arange(-rim_width, col_block + rim_width, dtype=jnp.int32)
    rows_inside = (ext_rows >= 0) & (ext_rows < lat_cells)
    cols_inside = (ext_cols >= 0) & (ext_cols < lon_cells)

    def slot_lookup(ghost_ids):
        return jnp.take(order_row, jnp.clip(ghost_ids, 0, ghost_count - 1))

    rim_slots = (
        slot_lookup(ext_cols),
        slot_lookup(lon_cells + ext_cols),
        slot_lookup(2 * lon_cells + ext_rows),
        slot_lookup(2 * lon_cells + lat_cells + ext_rows),
    )

    def extend(block_field):
        return with_halo(block_field, (("lat", 1), ("lon", 2)), rim_width)

    grown_field = extend(start_field)
    source_view = grown_field[
        :, rim_width : rim_width + row_block + 1, rim_width : rim_width + col_block + 1
    ]
    rows_given = corner_rows[0, 0]
    cols_given = corner_cols[0, 0]
    weights = corner_weights[0, 0]
    corners = (
        source_view[:, rows_given, cols_given],
        source_view[:, rows_given + 1, cols_given],
        source_view[:, rows_given, cols_given + 1],
        source_view[:, rows_given + 1, cols_given + 1],
    )
    corner_slots = jnp.transpose(jnp.stack(corners, axis=0), (2, 0, 1, 3))
    weight_slots = jnp.transpose(weights)
    partner_corners, partner_weights = swapped((corner_slots, weight_slots), "patch", 0)
    blank_rims = tuple(
        (jnp.zeros((3, rim_slot.shape[0], levels), jnp.float32) for rim_slot in rim_slots)
    )
    piece_corners = lax.all_gather(partner_corners, ("lat", "lon"), axis=0, tiled=True)
    piece_weights = lax.all_gather(partner_weights, ("lat", "lon"), axis=0, tiled=True)
    count_here = piece_corners.shape[0]
    outcome = []
    for rim_index in range(4):
        local_ids = rim_slots[rim_index]
        inside = (local_ids >= 0) & (local_ids < count_here)
        safe_ids = jnp.clip(local_ids, 0, count_here - 1)
        got_corners = jnp.transpose(jnp.take(piece_corners, safe_ids, axis=0), (1, 2, 0, 3))
        got_weights = jnp.transpose(jnp.take(piece_weights, safe_ids, axis=0))
        ghost_value = bilinear(
            got_weights, (got_corners[0], got_corners[1], got_corners[2], got_corners[3])
        )
        outcome.append(jnp.where(inside[None, :, None], ghost_value, blank_rims[rim_index]))
    rim_values = tuple(outcome)
    top_valid = cols_inside & (lat_index == 0)
    bottom_valid = cols_inside & (lat_index == lat_count - 1)
    left_valid = rows_inside & (lon_index == 0)
    right_valid = rows_inside & (lon_index == lon_count - 1)
    lower_row = rim_width + row_block
    right_col = rim_width + col_block

    def with_ghosts(grown):
        grown = grown.at[:, rim_width - 1].set(
            jnp.where(top_valid[None, :, None], rim_values[0], grown[:, rim_width - 1])
        )
        grown = grown.at[:, lower_row].set(
            jnp.where(bottom_valid[None, :, None], rim_values[1], grown[:, lower_row])
        )
        grown = grown.at[:, :, rim_width - 1].set(
            jnp.where(left_valid[None, :, None], rim_values[2], grown[:, :, rim_width - 1])
        )
        grown = grown.at[:, :, right_col].set(
            jnp.where(right_valid[None, :, None], rim_values[3], grown[:, :, right_col])
        )
        return grown

    def relax_colour(grown, colour, margin):
        first_cell = rim_width - margin
        row_end = rim_width + row_block + margin
        col_end = rim_width + col_block + margin
        loop_shift = 1 - margin
        region_rows = row_block + 2 * margin
        region_cols = col_block + 2 * margin
        padded = jnp.pad(grown, ((0, 0), (0, 0), (0, 0), (1, 1)))
        region_coefs = tuple(
            (
                face_coef[
                    loop_shift : loop_shift + region_rows, loop_shift : loop_shift + region_cols
                ]
                for face_coef in loop_coefs
            )
        )
        region_diag = loop_diag[
            loop_shift : loop_shift + region_rows, loop_shift : loop_shift + region_cols
        ]
        relaxed = (force_block + neighbour_sum(padded, region_coefs)) / region_diag
        chosen = (
            loop_parity[
                loop_shift : loop_shift + region_rows, loop_shift : loop_shift + region_cols
            ]
            == colour
        ) & loop_inside[
            loop_shift : loop_shift + region_rows, loop_shift : loop_shift + region_cols
        ]
        updated = jnp.where(chosen[None], relaxed, grown[:, first_cell:row_end, first_cell:col_end])
        return grown.at[:, first_cell:row_end, first_cell:col_end].set(updated)

    def interior(grown):
        return grown[:, rim_width : rim_width + row_block, rim_width : rim_width + col_block]

    current = with_ghosts(grown_field)
    for sweep_index in range(SWEEPS):
        if sweep_index > 0:
            current = with_ghosts(extend(interior(current)))
        current = relax_colour(current, 0, 0)
        current = with_ghosts(extend(interior(current)))
        current = relax_colour(current, 1, 0)
    smoothed = interior(current)
    grown_last = with_ghosts(extend(smoothed))
    padded_last = jnp.pad(grown_last, ((0, 0), (0, 0), (0, 0), (1, 1)))
    inner_coefs = tuple((face_coef[1:-1, 1:-1] for face_coef in loop_coefs))
    inner_diag = loop_diag[1:-1, 1:-1]
    residual_field = force_block - (inner_diag * smoothed - neighbour_sum(padded_last, inner_coefs))
    half_rows = row_block // 2
    half_cols = col_block // 2
    half_levels = levels // 2
    coarse_rhs = residual_field.reshape(3, half_rows, 2, half_cols, 2, half_levels, 2).mean(
        axis=(2, 4, 6)
    )
    coarse_visc = visc_ext.reshape(half_rows + 2, 2, half_cols + 2, 2, half_levels + 2, 2).mean(
        axis=(1, 3, 5)
    )
    coarse_coefs = face_terms(coarse_visc, 0.125)
    coarse_diag = diagonal_of(coarse_coefs)
    coarse_error = RELAX * coarse_rhs / coarse_diag
    for turn_index in range(COARSE - 1):
        coarse_grown = with_halo(coarse_error, (("lat", 1), ("lon", 2)), 1)
        coarse_pad = jnp.pad(coarse_grown, ((0, 0), (0, 0), (0, 0), (1, 1)))
        coarse_error = (
            coarse_error
            + RELAX
            * (coarse_rhs - (coarse_diag * coarse_error - neighbour_sum(coarse_pad, coarse_coefs)))
            / coarse_diag
        )
    correction = jnp.repeat(jnp.repeat(jnp.repeat(coarse_error, 2, axis=1), 2, axis=2), 2, axis=3)
    new_field = smoothed + correction
    return (new_field[None], residual_field[None])


def solution(mesh):
    placed = (
        P("patch", None, "lat", "lon", None),
        P("patch", None, "lat", "lon", None),
        P("patch", "lat", "lon", None),
        P("patch", None),
        P("patch", "lat", "lon"),
        P("patch", "lat", "lon"),
        P("patch", "lat", None, "lon"),
    )
    return jax.shard_map(
        per_device,
        mesh=mesh,
        in_specs=placed,
        out_specs=(P("patch", None, "lat", "lon", None), P("patch", None, "lat", "lon", None)),
        check_vma=False,
    )
```

profile of v0, /device:TPU:6, one launch (start us, length us, event | category | flops | bytes accessed | tf_op | source)
XLA Modules:
  0.0 1015.0 jit_solution(3838266500594718935)
XLA Ops:
  8.3 3.5 collective-permute-start.4
  13.2 4.2 collective-permute-done.5
  17.5 2.7 collective-permute-start.7
  20.9 4.5 collective-permute-done.7
  32.3 2.1 collective-permute-start.8
  35.1 3.5 collective-permute-start
  43.9 677.3 %all-gather = f32[256,3,4]{2,1,0:T(4,128)S(1)} all-gather(f32[1,3,4]{2,1,0:T(4,128)S(1)} %bitcast.274), channel_id=1, replica_groups=mesh['patch'=2,'lat'=8,'lon'=32] {'lat','lon'}, dimensions={0}, use_global_device_ids=true | all-gather | bytes 12336 | tf_op jit(solution)/shard_map/all_gather | solution.py:148
  724.7 3.6 collective-permute-start.2
  728.2 5.2 collective-permute-start.3
  733.7 2.7 collective-permute-start.6
  740.1 8.1 copy.123
  748.2 2.9 gather_fusion.11
  751.2 2.9 gather_fusion.8
  754.1 3.0 gather_fusion.17
  757.1 3.0 gather_fusion.14
  764.4 4.2 collective-permute-done.11
  768.7 4.4 collective-permute-start.12
  773.0 3.8 collective-permute-start.13
  776.9 4.1 collective-permute-done.13
  785.1 9.4 collective-permute-done.15
  794.6 1.9 collective-permute-start.16
  796.5 3.9 collective-permute-start.17
  800.5 4.0 collective-permute-done.17
  805.6 5.1 collective-permute-start.18
  812.1 4.2 collective-permute-done.19
  816.3 1.9 collective-permute-start.20
  818.3 4.1 collective-permute-start.21
  822.6 4.8 reshape.1395
  827.3 4.6 reduce_sum.19
  833.0 3.9 collective-permute-start.22
  838.4 4.2 collective-permute-done.23
  842.6 4.0 collective-permute-start.24
  848.7 5.9 collective-permute-done.25
  855.6 14.0 %reshape.1394 = f32[3,8,2,4,2,64,2]{6,5,4,3,2,1,0:T(8,128)} reshape(f32[3,16,8,128]{3,2,1,0:T(8,128)S(1)} %copy.142) | data formatting | bytes 393216 | tf_op jit(solution)/shard_map/reshape | solution.py:234
  869.6 5.5 reduce_sum.18
  875.2 3.1 collective-permute-start.26
  879.7 4.2 collective-permute-done.27
  883.9 1.9 collective-permute-start.28
  885.8 3.9 collective-permute-start.29
  889.8 3.7 collective-permute-done.29
  893.9 3.1 collective-permute-start.30
  898.3 4.2 collective-permute-done.31
  904.5 3.9 collective-permute-start.33
  908.4 3.8 collective-permute-done.33
  912.6 3.1 collective-permute-start.34
  917.0 4.2 collective-permute-done.35
  923.2 3.9 collective-permute-start.37
  927.1 3.8 collective-permute-done.37
  931.2 3.1 collective-permute-start.38
  935.7 4.2 collective-permute-done.39
  941.9 3.9 collective-permute-start.41
  945.8 3.8 collective-permute-done.41
  949.9 3.1 collective-permute-start.42
  954.4 4.2 collective-permute-done.43
  960.6 3.9 collective-permute-start.45
  964.5 3.8 collective-permute-done.45
  968.6 3.1 collective-permute-start.46
  973.1 4.2 collective-permute-done.47
  979.2 3.9 collective-permute-start.49
  983.2 3.8 collective-permute-done.49
  987.3 3.1 collective-permute-start.50
  991.8 4.2 collective-permute-done.51
  997.9 3.9 collective-permute-start.53
  1002.5 3.1 collective-permute-done.53
  (244 shorter events, 65.7 us)
Async XLA Ops:
  7.2 33.1 %copy-start = (s32[1,768]{1,0:T(1,128)S(1)}, s32[1,768]{1,0:T(1,128)}, u32[]{:S(2)}) copy-start(s32[1,768]{1,0:T(1,128)} %param.70) | copy-start | bytes 9220
  7.2 717.5 %copy-start.2 = (f32[1,16,8,128]{3,2,1,0:T(8,128)S(1)}, f32[1,16,8,128]{3,2,1,0:T(8,128)}, u32[]{:S(2)}) copy-start(f32[1,16,8,128]{3,2,1,0:T(8,128)} %param.69) | copy-start | bytes 196612
  7.2 732.9 %all-gather.3.cloned.1.call-start = ((), (), s32[]{:S(2)}) async-start(), calls=%async_computation | async-start | bytes 6316032 | tf_op jit(solution)/shard_map/all_gather | solution.py:147
  8.3 4.9 collective-permute-start.4
  11.8 5.6 collective-permute-start.5
  17.5 8.0 collective-permute-start.7
  27.9 3.1 collective-permute-start.9
  30.9 0.6 copy-start.3
  32.3 11.4 %collective-permute-start.8 = (f32[3,4]{0,1:T(4,128)S(1)}, f32[3,4]{0,1:T(4,128)S(1)}, u32[]{:S(2)}, u32[]{:S(2)}) collective-permute-start(f32[3,4]{0,1:T(4,128)S(1)} %bitcast.275), channel_id=1, source_target_pairs={{0,256},{256,0},{1,257},{257,1},{2,258},{258,2},{3,259},{259,3},{4... | collective-permute-start | bytes 152 | tf_op jit(solution)/shard_map/ppermute | solution.py:27
  35.1 689.5 %collective-permute-start = (f32[2,8,128]{2,1,0:T(8,128)S(1)}, f32[2,8,128]{2,1,0:T(8,128)S(1)}, u32[]{:S(2)}, u32[]{:S(2)}) collective-permute-start(f32[2,8,128]{2,1,0:T(8,128)S(1)} %get-tuple-element.390), channel_id=1, source_target_pairs={{0,32},{32,64},{64,96},{96,128},{128,160},{160,192},{192,224},{1,3... | collective-permute-start | bytes 24584 | tf_op jit(solution)/shard_map/ppermute | solution.py:18
  38.6 686.0 %collective-permute-start.1 = (f32[2,8,128]{2,1,0:T(8,128)S(1)}, f32[2,8,128]{2,1,0:T(8,128)S(1)}, u32[]{:S(2)}, u32[]{:S(2)}) collective-permute-start(f32[2,8,128]{2,1,0:T(8,128)S(1)} %get-tuple-element.391), channel_id=1, source_target_pairs={{32,0},{64,32},{96,64},{128,96},{160,128},{192,160},{224,192},{33,... | collective-permute-start | bytes 24584 | tf_op jit(solution)/shard_map/ppermute | solution.py:19
  724.7 11.8 %collective-permute-start.2 = (f32[20,2,128]{2,1,0:T(2,128)S(1)}, f32[20,2,128]{2,1,0:T(2,128)S(1)}, u32[]{:S(2)}, u32[]{:S(2)}) collective-permute-start(f32[20,2,128]{2,1,0:T(2,128)S(1)} %get-tuple-element.388), channel_id=1, source_target_pairs={{0,1},{1,2},{2,3},{3,4},{4,5},{5,6},{6,7},{7,8},{8,9},{9,10},{10,1... | collective-permute-start | bytes 61448 | tf_op jit(solution)/shard_map/ppermute | solution.py:18
  728.2 8.2 collective-permute-start.3
  733.7 6.3 collective-permute-start.6
  740.1 21.0 %copy-start.1 = (f32[1,3,16,8,128]{4,3,2,1,0:T(8,128)S(1)}, f32[1,3,16,8,128]{4,3,2,1,0:T(8,128)}, u32[]{:S(2)}) copy-start(f32[1,3,16,8,128]{4,3,2,1,0:T(8,128)} %param.68) | copy-start | bytes 589828
  761.7 2.7 collective-permute-start.10
  763.0 5.6 collective-permute-start.11
  768.7 8.2 collective-permute-start.12
  773.0 8.0 collective-permute-start.13
  782.1 3.1 collective-permute-start.14
  783.7 10.9 %collective-permute-start.15 = (f32[3,1,8,128]{3,0,2,1:T(4,128)S(1)}, f32[3,1,8,128]{3,0,2,1:T(4,128)S(1)}, u32[]{:S(2)}, u32[]{:S(2)}) collective-permute-start(f32[3,1,8,128]{3,0,2,1:T(4,128)S(1)} %get-tuple-element.368), channel_id=1, source_target_pairs={{32,0},{64,32},{96,64},{128,96},{160,128},{192,160},{224,192},{33,... | collective-permute-start | bytes 36872 | tf_op jit(solution)/shard_map/ppermute | solution.py:19
  794.6 5.9 collective-permute-start.16
  796.5 8.0 collective-permute-start.17
  805.6 6.6 collective-permute-start.18
  810.7 5.6 collective-permute-start.19
  816.3 15.6 %collective-permute-start.20 = (f32[3,18,1,128]{3,0,2,1:T(4,128)S(1)}, f32[3,18,1,128]{3,0,2,1:T(4,128)S(1)}, u32[]{:S(2)}, u32[]{:S(2)}) collective-permute-start(f32[3,18,1,128]{3,0,2,1:T(4,128)S(1)} %get-tuple-element.355), channel_id=1, source_target_pairs={{0,1},{1,2},{2,3},{3,4},{4,5},{5,6},{6,7},{7,8},{8,9},{9,10},{10,1... | collective-permute-start | bytes 82952 | tf_op jit(solution)/shard_map/ppermute | solution.py:18
  818.3 13.7 %collective-permute-start.21 = (f32[3,18,1,128]{3,0,2,1:T(4,128)S(1)}, f32[3,18,1,128]{3,0,2,1:T(4,128)S(1)}, u32[]{:S(2)}, u32[]{:S(2)}) collective-permute-start(f32[3,18,1,128]{3,0,2,1:T(4,128)S(1)} %get-tuple-element.356), channel_id=1, source_target_pairs={{1,0},{2,1},{3,2},{4,3},{5,4},{6,5},{7,6},{8,7},{9,8},{10,9},{11,1... | collective-permute-start | bytes 82952 | tf_op jit(solution)/shard_map/ppermute | solution.py:19
  833.0 5.4 collective-permute-start.22
  837.0 5.6 collective-permute-start.23
  842.6 6.1 collective-permute-start.24
  846.7 8.0 collective-permute-start.25
  875.2 4.5 collective-permute-start.26
  878.3 5.5 collective-permute-start.27
  883.9 5.9 collective-permute-start.28
  885.8 7.7 collective-permute-start.29
  893.9 4.5 collective-permute-start.30
  897.0 5.5 collective-permute-start.31
  902.6 5.9 collective-permute-start.32
  904.5 7.7 collective-permute-start.33
  912.6 4.5 collective-permute-start.34
  915.7 5.5 collective-permute-start.35
  921.3 5.9 collective-permute-start.36
  923.2 7.7 collective-permute-start.37
  931.2 4.5 collective-permute-start.38
  934.4 5.5 collective-permute-start.39
  939.9 5.9 collective-permute-start.40
  941.9 7.7 collective-permute-start.41
  949.9 4.5 collective-permute-start.42
  953.1 5.5 collective-permute-start.43
  958.6 5.9 collective-permute-start.44
  960.6 7.7 collective-permute-start.45
  968.6 4.5 collective-permute-start.46
  971.8 5.5 collective-permute-start.47
  977.3 5.9 collective-permute-start.48
  979.2 7.7 collective-permute-start.49
  987.3 4.5 collective-permute-start.50
  990.4 5.5 collective-permute-start.51
  996.0 6.6 collective-permute-start.52
  997.9 7.7 collective-permute-start.53
Sparse Core Ops, SparseCore 0:
  31.7 133.1 all-gather.2
where the time goes:
time: 1020 us
  blocking collectives  677 us (66%)
  starting transfers between devices  143 us (14%)
  waiting for transfers between devices  103 us (10%)
  local copies, waits for them, and re-layouts  55 us (5%)
  other arithmetic  21 us (2%)
  between operations  15.5 us (2%)
    all_gather x1, blocking collectives, per_device(): lax.all_gather(partner_weights, ('lat', 'lon'), axis=0, tiled=True)  677 us
    ppermute x26, waiting for transfers between devices, with_halo(): after = lax.ppermute(first, axis, down)  100 us
    ppermute x26, starting transfers between devices, with_halo(): before = lax.ppermute(last, axis, up)  72.8 us
    ppermute x26, starting transfers between devices, with_halo(): after = lax.ppermute(first, axis, down)  66 us
  transfers between devices with their start and end apart: 55, of which 30 were waited for; matrix products, arithmetic and copies ran while one was open for 2% of the time, Pallas kernels for 0%

commit v1 on v0

--- a/solution.py
+++ b/solution.py
@@ -145,7 +145,8 @@
         (jnp.zeros((3, rim_slot.shape[0], levels), jnp.float32) for rim_slot in rim_slots)
     )
     piece_corners = lax.all_gather(partner_corners, ("lat", "lon"), axis=0, tiled=True)
-    piece_weights = lax.all_gather(partner_weights, ("lat", "lon"), axis=0, tiled=True)
+    sent = jnp.stack([partner_weights] * lax.axis_size(("lat", "lon")))
+    piece_weights = jnp.concatenate(lax.all_to_all(sent, ("lat", "lon"), 0, 0), axis=0)
     count_here = piece_corners.shape[0]
     outcome = []
     for rim_index in range(4):

time: 1020 us -> 458 us (0.45)
  the two profiles are of different devices: /device:TPU:6 before, /device:TPU:198 now
where the time goes in v1:
time: 458 us; the launch traced here: 456 us
  waiting for transfers between devices  193 us (42%)
  starting transfers between devices  169 us (37%)
  local copies, waits for them, and re-layouts  57.4 us (13%)
  other arithmetic  21 us (5%)
  between operations  15.5 us (3%)
    ppermute x26, waiting for transfers between devices, with_halo(): after = lax.ppermute(first, axis, down)  110 us
    ppermute x26, starting transfers between devices, with_halo(): before = lax.ppermute(last, axis, up)  84.9 us
    all_gather x1, waiting for transfers between devices, per_device(): lax.all_gather(partner_corners, ('lat', 'lon'), axis=0, tiled=True)  75.8 us
    ppermute x26, starting transfers between devices, with_halo(): after = lax.ppermute(first, axis, down)  60.8 us
    all_to_all x1, starting transfers between devices, per_device(): lax.all_to_all(sent, ('lat', 'lon'), 0, 0)  19.1 us
    reshape x1, local copies, waits for them, and re-layouts, per_device(): residual_field.reshape(3, half_rows, 2, half_cols, 2, half_levels, 2)  14 us
    gather x4, local copies, waits for them, and re-layouts, per_device(): jnp.take(piece_corners, safe_ids, axis=0)  11.8 us
  transfers between devices with their start and end apart: 56, of which 31 were waited for; matrix products, arithmetic and copies ran while one was open for 5% of the time, Pallas kernels for 0%

profile of v1, /device:TPU:198, one launch (start us, length us, event | category | flops | bytes accessed | tf_op | source)
XLA Modules:
  0.0 455.6 jit_solution(16433542760269979192)
XLA Ops:
  8.3 3.5 collective-permute-start.4
  13.2 4.2 collective-permute-done.5
  17.5 2.7 collective-permute-start.7
  20.9 5.7 %collective-permute-done.7 = f32[3,18,1,128]{3,0,2,1:T(4,128)S(1)} collective-permute-done((f32[3,18,1,128]{3,0,2,1:T(4,128)S(1)}, f32[3,18,1,128]{3,0,2,1:T(4,128)S(1)}, u32[]{:S(2)}, u32[]{:S(2)}) %collective-permute-start.7) | collective-permute-done | bytes 27680 | tf_op jit(solution)/shard_map/ppermute | solution.py:19
  33.6 2.1 collective-permute-start.8
  36.4 3.5 collective-permute-start
  45.9 19.1 %all-to-all-start = ((f32[256,3,4]{1,2,0:T(4,128)}), f32[256,3,4]{1,2,0:T(4,128)S(1)}, u32[]{:S(2)}, u32[]{:S(2)}) async-start(f32[256,3,4]{1,2,0:T(4,128)} %stack.12), calls=%async_computation | async-start | bytes 1048576 | tf_op jit(solution)/shard_map/all_to_all | solution.py:149
  65.0 4.6 %collective-permute-start.2 = (f32[20,2,128]{2,1,0:T(2,128)S(1)}, f32[20,2,128]{2,1,0:T(2,128)S(1)}, u32[]{:S(2)}, u32[]{:S(2)}) collective-permute-start(f32[20,2,128]{2,1,0:T(2,128)S(1)} %get-tuple-element.388), channel_id=1, source_target_pairs={{0,1},{1,2},{2,3},{3,4},{4,5},{5,6},{6,7},{7,8},{8,9},{9,10},{10,1... | collective-permute-start | bytes 61448 | tf_op jit(solution)/shard_map/ppermute | solution.py:18
  71.5 7.4 %collective-permute-start.6 = (f32[3,18,1,128]{3,0,2,1:T(4,128)S(1)}, f32[3,18,1,128]{3,0,2,1:T(4,128)S(1)}, u32[]{:S(2)}, u32[]{:S(2)}) collective-permute-start(f32[3,18,1,128]{3,0,2,1:T(4,128)S(1)} %get-tuple-element.361), channel_id=1, source_target_pairs={{0,1},{1,2},{2,3},{3,4},{4,5},{5,6},{6,7},{7,8},{8,9},{9,10},{10,1... | collective-permute-start | bytes 82952 | tf_op jit(solution)/shard_map/ppermute | solution.py:18
  79.0 5.0 %all-to-all-done = f32[256,3,4]{1,2,0:T(4,128)S(1)} async-done(((f32[256,3,4]{1,2,0:T(4,128)}), f32[256,3,4]{1,2,0:T(4,128)S(1)}, u32[]{:S(2)}, u32[]{:S(2)}) %all-to-all-start) | async-done | bytes 12320 | tf_op jit(solution)/shard_map/all_to_all | solution.py:149
  91.8 75.8 %all-gather.2.cloned.1.call-done = f32[768,4,3,128]{3,2,0,1:T(4,128)} async-done(((f32[3,4,3,128]{3,2,0,1:T(4,128)}), f32[768,4,3,128]{3,2,0,1:T(4,128)}) %all-gather.2.cloned.1.call-update) | async-done | bytes 4718608 | tf_op jit(solution)/shard_map/all_gather | solution.py:147
  167.5 8.0 %copy.117 = f32[768,4,3,128]{3,1,2,0:T(4,128)} copy(f32[768,4,3,128]{3,2,0,1:T(4,128)} %all-gather.2.cloned.1.call-done) | data formatting | bytes 9437184 | tf_op jit(solution)/shard_map/all_gather | solution.py:147
  175.6 2.9 gather_fusion.11
  178.5 2.9 gather_fusion.8
  181.4 3.0 gather_fusion.17
  184.4 3.0 gather_fusion.14
  189.0 2.4 collective-permute-start.10
  192.8 4.2 collective-permute-done.11
  197.1 7.9 %collective-permute-start.12 = (f32[3,18,1,128]{3,0,2,1:T(4,128)S(1)}, f32[3,18,1,128]{3,0,2,1:T(4,128)S(1)}, u32[]{:S(2)}, u32[]{:S(2)}) collective-permute-start(f32[3,18,1,128]{3,0,2,1:T(4,128)S(1)} %get-tuple-element.359), channel_id=1, source_target_pairs={{0,1},{1,2},{2,3},{3,4},{4,5},{5,6},{6,7},{7,8},{8,9},{9,10},{10,1... | collective-permute-start | bytes 82952 | tf_op jit(solution)/shard_map/ppermute | solution.py:18
  206.9 7.2 %collective-permute-done.13 = f32[3,18,1,128]{3,0,2,1:T(4,128)S(1)} collective-permute-done((f32[3,18,1,128]{3,0,2,1:T(4,128)S(1)}, f32[3,18,1,128]{3,0,2,1:T(4,128)S(1)}, u32[]{:S(2)}, u32[]{:S(2)}) %collective-permute-start.13) | collective-permute-done | bytes 27680 | tf_op jit(solution)/shard_map/ppermute | solution.py:19
  215.2 3.4 collective-permute-start.14
  220.0 4.2 collective-permute-done.15
  226.2 3.9 collective-permute-start.17
  230.1 5.2 %collective-permute-done.17 = f32[3,18,1,128]{3,0,2,1:T(4,128)S(1)} collective-permute-done((f32[3,18,1,128]{3,0,2,1:T(4,128)S(1)}, f32[3,18,1,128]{3,0,2,1:T(4,128)S(1)}, u32[]{:S(2)}, u32[]{:S(2)}) %collective-permute-start.17) | collective-permute-done | bytes 27680 | tf_op jit(solution)/shard_map/ppermute | solution.py:19
  236.4 3.0 collective-permute-start.18
  240.9 4.2 collective-permute-done.19
  245.1 1.9 collective-permute-start.20
  247.0 4.1 collective-permute-start.21
  251.4 4.7 %reshape.1401 = f32[10,2,6,2,66,2]{5,4,1,0,3,2:T(8,128)} reshape(f32[20,12,132]{2,0,1:T(8,128)S(1)} %pad_maximum_fusion.8) | data formatting | bytes 253440 | tf_op jit(solution)/shard_map/reshape | solution.py:238
  256.1 4.6 %reduce_sum.19 = f32[10,6,66]{2,0,1:T(8,128)S(1)} reduce(f32[10,2,6,2,66,2]{5,4,1,0,3,2:T(8,128)} %reshape.1401, f32[]{:T(128)} %constant.689.clone.1), dimensions={1,3,5}, to_apply=%region_1.8 | reduce | flops 27720 | bytes 142564 | tf_op jit(solution)/shard_map/reduce_sum | solution.py:238
  261.8 3.9 collective-permute-start.22
  267.2 4.2 collective-permute-done.23
  271.4 5.2 %collective-permute-start.24 = (f32[3,18,1,128]{3,0,2,1:T(4,128)S(1)}, f32[3,18,1,128]{3,0,2,1:T(4,128)S(1)}, u32[]{:S(2)}, u32[]{:S(2)}) collective-permute-start(f32[3,18,1,128]{3,0,2,1:T(4,128)S(1)} %get-tuple-element.353), channel_id=1, source_target_pairs={{0,1},{1,2},{2,3},{3,4},{4,5},{5,6},{6,7},{7,8},{8,9},{9,10},{10,1... | collective-permute-start | bytes 82952 | tf_op jit(solution)/shard_map/ppermute | solution.py:18
  278.7 7.1 %collective-permute-done.25 = f32[3,18,1,128]{3,0,2,1:T(4,128)S(1)} collective-permute-done((f32[3,18,1,128]{3,0,2,1:T(4,128)S(1)}, f32[3,18,1,128]{3,0,2,1:T(4,128)S(1)}, u32[]{:S(2)}, u32[]{:S(2)}) %collective-permute-start.25) | collective-permute-done | bytes 27680 | tf_op jit(solution)/shard_map/ppermute | solution.py:19
  286.9 14.0 %reshape.1400 = f32[3,8,2,4,2,64,2]{6,5,4,3,2,1,0:T(8,128)} reshape(f32[3,16,8,128]{3,2,1,0:T(8,128)S(1)} %copy.136) | data formatting | bytes 393216 | tf_op jit(solution)/shard_map/reshape | solution.py:235
  300.8 5.5 %reduce_sum.18 = f32[3,8,4,64]{3,2,1,0:T(4,128)S(1)} reduce(f32[3,8,2,4,2,64,2]{6,5,4,3,2,1,0:T(8,128)} %reshape.1400, f32[]{:T(128)} %constant.689.clone.1), dimensions={2,4,6}, to_apply=%region_0.7 | reduce | flops 43008 | bytes 221188 | tf_op jit(solution)/shard_map/reduce_sum | solution.py:235
  306.4 3.3 collective-permute-start.26
  311.0 4.2 collective-permute-done.27
  317.1 3.9 collective-permute-start.29
  321.2 4.9 %collective-permute-done.29 = f32[3,10,1,64]{3,2,1,0:T(1,128)S(1)} collective-permute-done((f32[3,10,1,64]{3,2,1,0:T(1,128)S(1)}, f32[3,10,1,64]{3,2,1,0:T(1,128)S(1)}, u32[]{:S(2)}, u32[]{:S(2)}) %collective-permute-start.29) | collective-permute-done | bytes 7712 | tf_op jit(solution)/shard_map/ppermute | solution.py:19
  326.4 4.0 collective-permute-start.30
  331.7 4.2 collective-permute-done.31
  337.9 3.9 collective-permute-start.33
  341.8 5.0 %collective-permute-done.33 = f32[3,10,1,64]{3,2,1,0:T(1,128)S(1)} collective-permute-done((f32[3,10,1,64]{3,2,1,0:T(1,128)S(1)}, f32[3,10,1,64]{3,2,1,0:T(1,128)S(1)}, u32[]{:S(2)}, u32[]{:S(2)}) %collective-permute-start.33) | collective-permute-done | bytes 7712 | tf_op jit(solution)/shard_map/ppermute | solution.py:19
  347.1 3.1 collective-permute-start.34
  351.6 4.2 collective-permute-done.35
  357.7 3.9 collective-permute-start.37
  361.7 5.0 %collective-permute-done.37 = f32[3,10,1,64]{3,2,1,0:T(1,128)S(1)} collective-permute-done((f32[3,10,1,64]{3,2,1,0:T(1,128)S(1)}, f32[3,10,1,64]{3,2,1,0:T(1,128)S(1)}, u32[]{:S(2)}, u32[]{:S(2)}) %collective-permute-start.37) | collective-permute-done | bytes 7712 | tf_op jit(solution)/shard_map/ppermute | solution.py:19
  367.0 3.1 collective-permute-start.38
  371.5 4.2 collective-permute-done.39
  377.6 3.9 collective-permute-start.41
  381.6 5.0 %collective-permute-done.41 = f32[3,10,1,64]{3,2,1,0:T(1,128)S(1)} collective-permute-done((f32[3,10,1,64]{3,2,1,0:T(1,128)S(1)}, f32[3,10,1,64]{3,2,1,0:T(1,128)S(1)}, u32[]{:S(2)}, u32[]{:S(2)}) %collective-permute-start.41) | collective-permute-done | bytes 7712 | tf_op jit(solution)/shard_map/ppermute | solution.py:19
  386.9 3.1 collective-permute-start.42
  391.4 4.2 collective-permute-done.43
  397.5 3.9 collective-permute-start.45
  401.4 5.0 %collective-permute-done.45 = f32[3,10,1,64]{3,2,1,0:T(1,128)S(1)} collective-permute-done((f32[3,10,1,64]{3,2,1,0:T(1,128)S(1)}, f32[3,10,1,64]{3,2,1,0:T(1,128)S(1)}, u32[]{:S(2)}, u32[]{:S(2)}) %collective-permute-start.45) | collective-permute-done | bytes 7712 | tf_op jit(solution)/shard_map/ppermute | solution.py:19
  406.8 3.1 collective-permute-start.46
  411.2 4.2 collective-permute-done.47
  417.4 3.9 collective-permute-start.49
  421.3 5.0 %collective-permute-done.49 = f32[3,10,1,64]{3,2,1,0:T(1,128)S(1)} collective-permute-done((f32[3,10,1,64]{3,2,1,0:T(1,128)S(1)}, f32[3,10,1,64]{3,2,1,0:T(1,128)S(1)}, u32[]{:S(2)}, u32[]{:S(2)}) %collective-permute-start.49) | collective-permute-done | bytes 7712 | tf_op jit(solution)/shard_map/ppermute | solution.py:19
  426.7 3.1 collective-permute-start.50
  431.1 4.2 collective-permute-done.51
  437.3 3.9 collective-permute-start.53
  441.9 4.3 collective-permute-done.53
  (246 shorter events, 71.7 us)
Async XLA Ops:
  7.2 34.3 %copy-start = (s32[1,768]{1,0:T(1,128)S(1)}, s32[1,768]{1,0:T(1,128)}, u32[]{:S(2)}) copy-start(s32[1,768]{1,0:T(1,128)} %param.70) | copy-start | bytes 9220
  7.2 57.8 %copy-start.2 = (f32[1,16,8,128]{3,2,1,0:T(8,128)S(1)}, f32[1,16,8,128]{3,2,1,0:T(8,128)}, u32[]{:S(2)}) copy-start(f32[1,16,8,128]{3,2,1,0:T(8,128)} %param.69) | copy-start | bytes 196612
  7.2 160.3 %all-gather.2.cloned.1.call-start = ((), (), s32[]{:S(2)}) async-start(), calls=%async_computation.1 | async-start | bytes 6316032 | tf_op jit(solution)/shard_map/all_gather | solution.py:147
  8.3 4.9 %collective-permute-start.4 = (f32[3,1,8,128]{3,0,2,1:T(4,128)S(1)}, f32[3,1,8,128]{3,0,2,1:T(4,128)S(1)}, u32[]{:S(2)}, u32[]{:S(2)}) collective-permute-start(f32[3,1,8,128]{3,0,2,1:T(4,128)S(1)} %get-tuple-element.371), channel_id=1, source_target_pairs={{0,32},{32,64},{64,96},{96,128},{128,160},{160,192},{192,224},{1,3... | collective-permute-start | bytes 36872 | tf_op jit(solution)/shard_map/ppermute | solution.py:18
  11.8 5.6 %collective-permute-start.5 = (f32[3,1,8,128]{3,0,2,1:T(4,128)S(1)}, f32[3,1,8,128]{3,0,2,1:T(4,128)S(1)}, u32[]{:S(2)}, u32[]{:S(2)}) collective-permute-start(f32[3,1,8,128]{3,0,2,1:T(4,128)S(1)} %get-tuple-element.372), channel_id=1, source_target_pairs={{32,0},{64,32},{96,64},{128,96},{160,128},{192,160},{224,192},{33,... | collective-permute-start | bytes 36872 | tf_op jit(solution)/shard_map/ppermute | solution.py:19
  17.5 9.2 %collective-permute-start.7 = (f32[3,18,1,128]{3,0,2,1:T(4,128)S(1)}, f32[3,18,1,128]{3,0,2,1:T(4,128)S(1)}, u32[]{:S(2)}, u32[]{:S(2)}) collective-permute-start(f32[3,18,1,128]{3,0,2,1:T(4,128)S(1)} %get-tuple-element.362), channel_id=1, source_target_pairs={{1,0},{2,1},{3,2},{4,3},{5,4},{6,5},{7,6},{8,7},{9,8},{10,9},{11,1... | collective-permute-start | bytes 82952 | tf_op jit(solution)/shard_map/ppermute | solution.py:19
  29.1 3.1 collective-permute-start.9
  32.2 0.6 copy-start.3
  33.6 11.4 %collective-permute-start.8 = (f32[3,4]{0,1:T(4,128)S(1)}, f32[3,4]{0,1:T(4,128)S(1)}, u32[]{:S(2)}, u32[]{:S(2)}) collective-permute-start(f32[3,4]{0,1:T(4,128)S(1)} %bitcast.273), channel_id=1, source_target_pairs={{0,256},{256,0},{1,257},{257,1},{2,258},{258,2},{3,259},{259,3},{4... | collective-permute-start | bytes 152 | tf_op jit(solution)/shard_map/ppermute | solution.py:27
  36.4 28.6 %collective-permute-start = (f32[2,8,128]{2,1,0:T(8,128)S(1)}, f32[2,8,128]{2,1,0:T(8,128)S(1)}, u32[]{:S(2)}, u32[]{:S(2)}) collective-permute-start(f32[2,8,128]{2,1,0:T(8,128)S(1)} %get-tuple-element.390), channel_id=1, source_target_pairs={{0,32},{32,64},{64,96},{96,128},{128,160},{160,192},{192,224},{1,3... | collective-permute-start | bytes 24584 | tf_op jit(solution)/shard_map/ppermute | solution.py:18
  39.8 25.1 %collective-permute-start.1 = (f32[2,8,128]{2,1,0:T(8,128)S(1)}, f32[2,8,128]{2,1,0:T(8,128)S(1)}, u32[]{:S(2)}, u32[]{:S(2)}) collective-permute-start(f32[2,8,128]{2,1,0:T(8,128)S(1)} %get-tuple-element.391), channel_id=1, source_target_pairs={{32,0},{64,32},{96,64},{128,96},{160,128},{192,160},{224,192},{33,... | collective-permute-start | bytes 24584 | tf_op jit(solution)/shard_map/ppermute | solution.py:19
  45.9 38.1 %all-to-all-start = ((f32[256,3,4]{1,2,0:T(4,128)}), f32[256,3,4]{1,2,0:T(4,128)S(1)}, u32[]{:S(2)}, u32[]{:S(2)}) async-start(f32[256,3,4]{1,2,0:T(4,128)} %stack.12), calls=%async_computation | async-start | bytes 1048576 | tf_op jit(solution)/shard_map/all_to_all | solution.py:149
  65.0 24.3 %collective-permute-start.2 = (f32[20,2,128]{2,1,0:T(2,128)S(1)}, f32[20,2,128]{2,1,0:T(2,128)S(1)}, u32[]{:S(2)}, u32[]{:S(2)}) collective-permute-start(f32[20,2,128]{2,1,0:T(2,128)S(1)} %get-tuple-element.388), channel_id=1, source_target_pairs={{0,1},{1,2},{2,3},{3,4},{4,5},{5,6},{6,7},{7,8},{8,9},{9,10},{10,1... | collective-permute-start | bytes 61448 | tf_op jit(solution)/shard_map/ppermute | solution.py:18
  69.6 19.7 %collective-permute-start.3 = (f32[20,2,128]{2,1,0:T(2,128)S(1)}, f32[20,2,128]{2,1,0:T(2,128)S(1)}, u32[]{:S(2)}, u32[]{:S(2)}) collective-permute-start(f32[20,2,128]{2,1,0:T(2,128)S(1)} %get-tuple-element.389), channel_id=1, source_target_pairs={{1,0},{2,1},{3,2},{4,3},{5,4},{6,5},{7,6},{8,7},{9,8},{10,9},{11,1... | collective-permute-start | bytes 61448 | tf_op jit(solution)/shard_map/ppermute | solution.py:19
  71.5 20.1 %collective-permute-start.6 = (f32[3,18,1,128]{3,0,2,1:T(4,128)S(1)}, f32[3,18,1,128]{3,0,2,1:T(4,128)S(1)}, u32[]{:S(2)}, u32[]{:S(2)}) collective-permute-start(f32[3,18,1,128]{3,0,2,1:T(4,128)S(1)} %get-tuple-element.361), channel_id=1, source_target_pairs={{0,1},{1,2},{2,3},{3,4},{4,5},{5,6},{6,7},{7,8},{8,9},{9,10},{10,1... | collective-permute-start | bytes 82952 | tf_op jit(solution)/shard_map/ppermute | solution.py:18
  91.7 96.7 %copy-start.1 = (f32[1,3,16,8,128]{4,3,2,1,0:T(8,128)S(1)}, f32[1,3,16,8,128]{4,3,2,1,0:T(8,128)}, u32[]{:S(2)}) copy-start(f32[1,3,16,8,128]{4,3,2,1,0:T(8,128)} %param.68) | copy-start | bytes 589828
  189.0 3.8 collective-permute-start.10
  191.4 5.6 %collective-permute-start.11 = (f32[3,1,8,128]{3,0,2,1:T(4,128)S(1)}, f32[3,1,8,128]{3,0,2,1:T(4,128)S(1)}, u32[]{:S(2)}, u32[]{:S(2)}) collective-permute-start(f32[3,1,8,128]{3,0,2,1:T(4,128)S(1)} %get-tuple-element.370), channel_id=1, source_target_pairs={{32,0},{64,32},{96,64},{128,96},{160,128},{192,160},{224,192},{33,... | collective-permute-start | bytes 36872 | tf_op jit(solution)/shard_map/ppermute | solution.py:19
  197.1 9.8 %collective-permute-start.12 = (f32[3,18,1,128]{3,0,2,1:T(4,128)S(1)}, f32[3,18,1,128]{3,0,2,1:T(4,128)S(1)}, u32[]{:S(2)}, u32[]{:S(2)}) collective-permute-start(f32[3,18,1,128]{3,0,2,1:T(4,128)S(1)} %get-tuple-element.359), channel_id=1, source_target_pairs={{0,1},{1,2},{2,3},{3,4},{4,5},{5,6},{6,7},{7,8},{8,9},{9,10},{10,1... | collective-permute-start | bytes 82952 | tf_op jit(solution)/shard_map/ppermute | solution.py:18
  205.0 9.2 %collective-permute-start.13 = (f32[3,18,1,128]{3,0,2,1:T(4,128)S(1)}, f32[3,18,1,128]{3,0,2,1:T(4,128)S(1)}, u32[]{:S(2)}, u32[]{:S(2)}) collective-permute-start(f32[3,18,1,128]{3,0,2,1:T(4,128)S(1)} %get-tuple-element.360), channel_id=1, source_target_pairs={{1,0},{2,1},{3,2},{4,3},{5,4},{6,5},{7,6},{8,7},{9,8},{10,9},{11,1... | collective-permute-start | bytes 82952 | tf_op jit(solution)/shard_map/ppermute | solution.py:19
  215.2 4.8 %collective-permute-start.14 = (f32[3,1,8,128]{3,0,2,1:T(4,128)S(1)}, f32[3,1,8,128]{3,0,2,1:T(4,128)S(1)}, u32[]{:S(2)}, u32[]{:S(2)}) collective-permute-start(f32[3,1,8,128]{3,0,2,1:T(4,128)S(1)} %get-tuple-element.367), channel_id=1, source_target_pairs={{0,32},{32,64},{64,96},{96,128},{128,160},{160,192},{192,224},{1,3... | collective-permute-start | bytes 36872 | tf_op jit(solution)/shard_map/ppermute | solution.py:18
  218.6 5.6 %collective-permute-start.15 = (f32[3,1,8,128]{3,0,2,1:T(4,128)S(1)}, f32[3,1,8,128]{3,0,2,1:T(4,128)S(1)}, u32[]{:S(2)}, u32[]{:S(2)}) collective-permute-start(f32[3,1,8,128]{3,0,2,1:T(4,128)S(1)} %get-tuple-element.368), channel_id=1, source_target_pairs={{32,0},{64,32},{96,64},{128,96},{160,128},{192,160},{224,192},{33,... | collective-permute-start | bytes 36872 | tf_op jit(solution)/shard_map/ppermute | solution.py:19
  224.3 5.9 %collective-permute-start.16 = (f32[3,18,1,128]{3,0,2,1:T(4,128)S(1)}, f32[3,18,1,128]{3,0,2,1:T(4,128)S(1)}, u32[]{:S(2)}, u32[]{:S(2)}) collective-permute-start(f32[3,18,1,128]{3,0,2,1:T(4,128)S(1)} %get-tuple-element.357), channel_id=1, source_target_pairs={{0,1},{1,2},{2,3},{3,4},{4,5},{5,6},{6,7},{7,8},{8,9},{9,10},{10,1... | collective-permute-start | bytes 82952 | tf_op jit(solution)/shard_map/ppermute | solution.py:18
  226.2 9.2 %collective-permute-start.17 = (f32[3,18,1,128]{3,0,2,1:T(4,128)S(1)}, f32[3,18,1,128]{3,0,2,1:T(4,128)S(1)}, u32[]{:S(2)}, u32[]{:S(2)}) collective-permute-start(f32[3,18,1,128]{3,0,2,1:T(4,128)S(1)} %get-tuple-element.358), channel_id=1, source_target_pairs={{1,0},{2,1},{3,2},{4,3},{5,4},{6,5},{7,6},{8,7},{9,8},{10,9},{11,1... | collective-permute-start | bytes 82952 | tf_op jit(solution)/shard_map/ppermute | solution.py:19
  236.4 4.4 collective-permute-start.18
  239.5 5.6 %collective-permute-start.19 = (f32[3,1,8,128]{3,0,2,1:T(4,128)S(1)}, f32[3,1,8,128]{3,0,2,1:T(4,128)S(1)}, u32[]{:S(2)}, u32[]{:S(2)}) collective-permute-start(f32[3,1,8,128]{3,0,2,1:T(4,128)S(1)} %get-tuple-element.366), channel_id=1, source_target_pairs={{32,0},{64,32},{96,64},{128,96},{160,128},{192,160},{224,192},{33,... | collective-permute-start | bytes 36872 | tf_op jit(solution)/shard_map/ppermute | solution.py:19
  245.1 15.6 %collective-permute-start.20 = (f32[3,18,1,128]{3,0,2,1:T(4,128)S(1)}, f32[3,18,1,128]{3,0,2,1:T(4,128)S(1)}, u32[]{:S(2)}, u32[]{:S(2)}) collective-permute-start(f32[3,18,1,128]{3,0,2,1:T(4,128)S(1)} %get-tuple-element.355), channel_id=1, source_target_pairs={{0,1},{1,2},{2,3},{3,4},{4,5},{5,6},{6,7},{7,8},{8,9},{9,10},{10,1... | collective-permute-start | bytes 82952 | tf_op jit(solution)/shard_map/ppermute | solution.py:18
  247.0 13.7 %collective-permute-start.21 = (f32[3,18,1,128]{3,0,2,1:T(4,128)S(1)}, f32[3,18,1,128]{3,0,2,1:T(4,128)S(1)}, u32[]{:S(2)}, u32[]{:S(2)}) collective-permute-start(f32[3,18,1,128]{3,0,2,1:T(4,128)S(1)} %get-tuple-element.356), channel_id=1, source_target_pairs={{1,0},{2,1},{3,2},{4,3},{5,4},{6,5},{7,6},{8,7},{9,8},{10,9},{11,1... | collective-permute-start | bytes 82952 | tf_op jit(solution)/shard_map/ppermute | solution.py:19
  261.8 5.4 %collective-permute-start.22 = (f32[3,1,8,128]{3,0,2,1:T(4,128)S(1)}, f32[3,1,8,128]{3,0,2,1:T(4,128)S(1)}, u32[]{:S(2)}, u32[]{:S(2)}) collective-permute-start(f32[3,1,8,128]{3,0,2,1:T(4,128)S(1)} %get-tuple-element.363), channel_id=1, source_target_pairs={{0,32},{32,64},{64,96},{96,128},{128,160},{160,192},{192,224},{1,3... | collective-permute-start | bytes 36872 | tf_op jit(solution)/shard_map/ppermute | solution.py:18
  265.7 5.6 %collective-permute-start.23 = (f32[3,1,8,128]{3,0,2,1:T(4,128)S(1)}, f32[3,1,8,128]{3,0,2,1:T(4,128)S(1)}, u32[]{:S(2)}, u32[]{:S(2)}) collective-permute-start(f32[3,1,8,128]{3,0,2,1:T(4,128)S(1)} %get-tuple-element.364), channel_id=1, source_target_pairs={{32,0},{64,32},{96,64},{128,96},{160,128},{192,160},{224,192},{33,... | collective-permute-start | bytes 36872 | tf_op jit(solution)/shard_map/ppermute | solution.py:19
  271.4 7.3 %collective-permute-start.24 = (f32[3,18,1,128]{3,0,2,1:T(4,128)S(1)}, f32[3,18,1,128]{3,0,2,1:T(4,128)S(1)}, u32[]{:S(2)}, u32[]{:S(2)}) collective-permute-start(f32[3,18,1,128]{3,0,2,1:T(4,128)S(1)} %get-tuple-element.353), channel_id=1, source_target_pairs={{0,1},{1,2},{2,3},{3,4},{4,5},{5,6},{6,7},{7,8},{8,9},{9,10},{10,1... | collective-permute-start | bytes 82952 | tf_op jit(solution)/shard_map/ppermute | solution.py:18
  276.7 9.2 %collective-permute-start.25 = (f32[3,18,1,128]{3,0,2,1:T(4,128)S(1)}, f32[3,18,1,128]{3,0,2,1:T(4,128)S(1)}, u32[]{:S(2)}, u32[]{:S(2)}) collective-permute-start(f32[3,18,1,128]{3,0,2,1:T(4,128)S(1)} %get-tuple-element.354), channel_id=1, source_target_pairs={{1,0},{2,1},{3,2},{4,3},{5,4},{6,5},{7,6},{8,7},{9,8},{10,9},{11,1... | collective-permute-start | bytes 82952 | tf_op jit(solution)/shard_map/ppermute | solution.py:19
  306.4 4.6 %collective-permute-start.26 = (f32[3,1,4,64]{3,2,1,0:T(4,128)S(1)}, f32[3,1,4,64]{3,2,1,0:T(4,128)S(1)}, u32[]{:S(2)}, u32[]{:S(2)}) collective-permute-start(f32[3,1,4,64]{3,2,1,0:T(4,128)S(1)} %get-tuple-element.418), channel_id=1, source_target_pairs={{0,32},{32,64},{64,96},{96,128},{128,160},{160,192},{192,224},{1,3... | collective-permute-start | bytes 9224 | tf_op jit(solution)/shard_map/ppermute | solution.py:18
  309.7 5.5 %collective-permute-start.27 = (f32[3,1,4,64]{3,2,1,0:T(4,128)S(1)}, f32[3,1,4,64]{3,2,1,0:T(4,128)S(1)}, u32[]{:S(2)}, u32[]{:S(2)}) collective-permute-start(f32[3,1,4,64]{3,2,1,0:T(4,128)S(1)} %get-tuple-element.419), channel_id=1, source_target_pairs={{32,0},{64,32},{96,64},{128,96},{160,128},{192,160},{224,192},{33,... | collective-permute-start | bytes 9224 | tf_op jit(solution)/shard_map/ppermute | solution.py:19
  315.2 5.9 %collective-permute-start.28 = (f32[3,10,1,64]{3,2,1,0:T(1,128)S(1)}, f32[3,10,1,64]{3,2,1,0:T(1,128)S(1)}, u32[]{:S(2)}, u32[]{:S(2)}) collective-permute-start(f32[3,10,1,64]{3,2,1,0:T(1,128)S(1)} %get-tuple-element.404), channel_id=1, source_target_pairs={{0,1},{1,2},{2,3},{3,4},{4,5},{5,6},{6,7},{7,8},{8,9},{9,10},{10,1... | collective-permute-start | bytes 23048 | tf_op jit(solution)/shard_map/ppermute | solution.py:18
  317.1 8.9 %collective-permute-start.29 = (f32[3,10,1,64]{3,2,1,0:T(1,128)S(1)}, f32[3,10,1,64]{3,2,1,0:T(1,128)S(1)}, u32[]{:S(2)}, u32[]{:S(2)}) collective-permute-start(f32[3,10,1,64]{3,2,1,0:T(1,128)S(1)} %get-tuple-element.405), channel_id=1, source_target_pairs={{1,0},{2,1},{3,2},{4,3},{5,4},{6,5},{7,6},{8,7},{9,8},{10,9},{11,1... | collective-permute-start | bytes 23048 | tf_op jit(solution)/shard_map/ppermute | solution.py:19
  326.4 5.3 %collective-permute-start.30 = (f32[3,1,4,64]{3,2,1,0:T(4,128)S(1)}, f32[3,1,4,64]{3,2,1,0:T(4,128)S(1)}, u32[]{:S(2)}, u32[]{:S(2)}) collective-permute-start(f32[3,1,4,64]{3,2,1,0:T(4,128)S(1)} %get-tuple-element.416), channel_id=1, source_target_pairs={{0,32},{32,64},{64,96},{96,128},{128,160},{160,192},{192,224},{1,3... | collective-permute-start | bytes 9224 | tf_op jit(solution)/shard_map/ppermute | solution.py:18
  330.4 5.5 %collective-permute-start.31 = (f32[3,1,4,64]{3,2,1,0:T(4,128)S(1)}, f32[3,1,4,64]{3,2,1,0:T(4,128)S(1)}, u32[]{:S(2)}, u32[]{:S(2)}) collective-permute-start(f32[3,1,4,64]{3,2,1,0:T(4,128)S(1)} %get-tuple-element.417), channel_id=1, source_target_pairs={{32,0},{64,32},{96,64},{128,96},{160,128},{192,160},{224,192},{33,... | collective-permute-start | bytes 9224 | tf_op jit(solution)/shard_map/ppermute | solution.py:19
  335.9 5.9 %collective-permute-start.32 = (f32[3,10,1,64]{3,2,1,0:T(1,128)S(1)}, f32[3,10,1,64]{3,2,1,0:T(1,128)S(1)}, u32[]{:S(2)}, u32[]{:S(2)}) collective-permute-start(f32[3,10,1,64]{3,2,1,0:T(1,128)S(1)} %get-tuple-element.402), channel_id=1, source_target_pairs={{0,1},{1,2},{2,3},{3,4},{4,5},{5,6},{6,7},{7,8},{8,9},{9,10},{10,1... | collective-permute-start | bytes 23048 | tf_op jit(solution)/shard_map/ppermute | solution.py:18
  337.9 8.9 %collective-permute-start.33 = (f32[3,10,1,64]{3,2,1,0:T(1,128)S(1)}, f32[3,10,1,64]{3,2,1,0:T(1,128)S(1)}, u32[]{:S(2)}, u32[]{:S(2)}) collective-permute-start(f32[3,10,1,64]{3,2,1,0:T(1,128)S(1)} %get-tuple-element.403), channel_id=1, source_target_pairs={{1,0},{2,1},{3,2},{4,3},{5,4},{6,5},{7,6},{8,7},{9,8},{10,9},{11,1... | collective-permute-start | bytes 23048 | tf_op jit(solution)/shard_map/ppermute | solution.py:19
  347.1 4.4 collective-permute-start.34
  350.2 5.5 %collective-permute-start.35 = (f32[3,1,4,64]{3,2,1,0:T(4,128)S(1)}, f32[3,1,4,64]{3,2,1,0:T(4,128)S(1)}, u32[]{:S(2)}, u32[]{:S(2)}) collective-permute-start(f32[3,1,4,64]{3,2,1,0:T(4,128)S(1)} %get-tuple-element.415), channel_id=1, source_target_pairs={{32,0},{64,32},{96,64},{128,96},{160,128},{192,160},{224,192},{33,... | collective-permute-start | bytes 9224 | tf_op jit(solution)/shard_map/ppermute | solution.py:19
  355.8 5.9 %collective-permute-start.36 = (f32[3,10,1,64]{3,2,1,0:T(1,128)S(1)}, f32[3,10,1,64]{3,2,1,0:T(1,128)S(1)}, u32[]{:S(2)}, u32[]{:S(2)}) collective-permute-start(f32[3,10,1,64]{3,2,1,0:T(1,128)S(1)} %get-tuple-element.400), channel_id=1, source_target_pairs={{0,1},{1,2},{2,3},{3,4},{4,5},{5,6},{6,7},{7,8},{8,9},{9,10},{10,1... | collective-permute-start | bytes 23048 | tf_op jit(solution)/shard_map/ppermute | solution.py:18
  357.7 8.9 %collective-permute-start.37 = (f32[3,10,1,64]{3,2,1,0:T(1,128)S(1)}, f32[3,10,1,64]{3,2,1,0:T(1,128)S(1)}, u32[]{:S(2)}, u32[]{:S(2)}) collective-permute-start(f32[3,10,1,64]{3,2,1,0:T(1,128)S(1)} %get-tuple-element.401), channel_id=1, source_target_pairs={{1,0},{2,1},{3,2},{4,3},{5,4},{6,5},{7,6},{8,7},{9,8},{10,9},{11,1... | collective-permute-start | bytes 23048 | tf_op jit(solution)/shard_map/ppermute | solution.py:19
  367.0 4.5 collective-permute-start.38
  370.1 5.5 %collective-permute-start.39 = (f32[3,1,4,64]{3,2,1,0:T(4,128)S(1)}, f32[3,1,4,64]{3,2,1,0:T(4,128)S(1)}, u32[]{:S(2)}, u32[]{:S(2)}) collective-permute-start(f32[3,1,4,64]{3,2,1,0:T(4,128)S(1)} %get-tuple-element.413), channel_id=1, source_target_pairs={{32,0},{64,32},{96,64},{128,96},{160,128},{192,160},{224,192},{33,... | collective-permute-start | bytes 9224 | tf_op jit(solution)/shard_map/ppermute | solution.py:19
  375.7 5.9 %collective-permute-start.40 = (f32[3,10,1,64]{3,2,1,0:T(1,128)S(1)}, f32[3,10,1,64]{3,2,1,0:T(1,128)S(1)}, u32[]{:S(2)}, u32[]{:S(2)}) collective-permute-start(f32[3,10,1,64]{3,2,1,0:T(1,128)S(1)} %get-tuple-element.398), channel_id=1, source_target_pairs={{0,1},{1,2},{2,3},{3,4},{4,5},{5,6},{6,7},{7,8},{8,9},{9,10},{10,1... | collective-permute-start | bytes 23048 | tf_op jit(solution)/shard_map/ppermute | solution.py:18
  377.6 8.9 %collective-permute-start.41 = (f32[3,10,1,64]{3,2,1,0:T(1,128)S(1)}, f32[3,10,1,64]{3,2,1,0:T(1,128)S(1)}, u32[]{:S(2)}, u32[]{:S(2)}) collective-permute-start(f32[3,10,1,64]{3,2,1,0:T(1,128)S(1)} %get-tuple-element.399), channel_id=1, source_target_pairs={{1,0},{2,1},{3,2},{4,3},{5,4},{6,5},{7,6},{8,7},{9,8},{10,9},{11,1... | collective-permute-start | bytes 23048 | tf_op jit(solution)/shard_map/ppermute | solution.py:19
  386.9 4.5 collective-permute-start.42
  390.0 5.5 %collective-permute-start.43 = (f32[3,1,4,64]{3,2,1,0:T(4,128)S(1)}, f32[3,1,4,64]{3,2,1,0:T(4,128)S(1)}, u32[]{:S(2)}, u32[]{:S(2)}) collective-permute-start(f32[3,1,4,64]{3,2,1,0:T(4,128)S(1)} %get-tuple-element.411), channel_id=1, source_target_pairs={{32,0},{64,32},{96,64},{128,96},{160,128},{192,160},{224,192},{33,... | collective-permute-start | bytes 9224 | tf_op jit(solution)/shard_map/ppermute | solution.py:19
  395.6 5.9 %collective-permute-start.44 = (f32[3,10,1,64]{3,2,1,0:T(1,128)S(1)}, f32[3,10,1,64]{3,2,1,0:T(1,128)S(1)}, u32[]{:S(2)}, u32[]{:S(2)}) collective-permute-start(f32[3,10,1,64]{3,2,1,0:T(1,128)S(1)} %get-tuple-element.396), channel_id=1, source_target_pairs={{0,1},{1,2},{2,3},{3,4},{4,5},{5,6},{6,7},{7,8},{8,9},{9,10},{10,1... | collective-permute-start | bytes 23048 | tf_op jit(solution)/shard_map/ppermute | solution.py:18
  397.5 8.9 %collective-permute-start.45 = (f32[3,10,1,64]{3,2,1,0:T(1,128)S(1)}, f32[3,10,1,64]{3,2,1,0:T(1,128)S(1)}, u32[]{:S(2)}, u32[]{:S(2)}) collective-permute-start(f32[3,10,1,64]{3,2,1,0:T(1,128)S(1)} %get-tuple-element.397), channel_id=1, source_target_pairs={{1,0},{2,1},{3,2},{4,3},{5,4},{6,5},{7,6},{8,7},{9,8},{10,9},{11,1... | collective-permute-start | bytes 23048 | tf_op jit(solution)/shard_map/ppermute | solution.py:19
  406.8 4.5 collective-permute-start.46
  409.9 5.5 %collective-permute-start.47 = (f32[3,1,4,64]{3,2,1,0:T(4,128)S(1)}, f32[3,1,4,64]{3,2,1,0:T(4,128)S(1)}, u32[]{:S(2)}, u32[]{:S(2)}) collective-permute-start(f32[3,1,4,64]{3,2,1,0:T(4,128)S(1)} %get-tuple-element.409), channel_id=1, source_target_pairs={{32,0},{64,32},{96,64},{128,96},{160,128},{192,160},{224,192},{33,... | collective-permute-start | bytes 9224 | tf_op jit(solution)/shard_map/ppermute | solution.py:19
  415.5 5.9 %collective-permute-start.48 = (f32[3,10,1,64]{3,2,1,0:T(1,128)S(1)}, f32[3,10,1,64]{3,2,1,0:T(1,128)S(1)}, u32[]{:S(2)}, u32[]{:S(2)}) collective-permute-start(f32[3,10,1,64]{3,2,1,0:T(1,128)S(1)} %get-tuple-element.394), channel_id=1, source_target_pairs={{0,1},{1,2},{2,3},{3,4},{4,5},{5,6},{6,7},{7,8},{8,9},{9,10},{10,1... | collective-permute-start | bytes 23048 | tf_op jit(solution)/shard_map/ppermute | solution.py:18
  417.4 8.9 %collective-permute-start.49 = (f32[3,10,1,64]{3,2,1,0:T(1,128)S(1)}, f32[3,10,1,64]{3,2,1,0:T(1,128)S(1)}, u32[]{:S(2)}, u32[]{:S(2)}) collective-permute-start(f32[3,10,1,64]{3,2,1,0:T(1,128)S(1)} %get-tuple-element.395), channel_id=1, source_target_pairs={{1,0},{2,1},{3,2},{4,3},{5,4},{6,5},{7,6},{8,7},{9,8},{10,9},{11,1... | collective-permute-start | bytes 23048 | tf_op jit(solution)/shard_map/ppermute | solution.py:19
  426.7 4.5 collective-permute-start.50
  429.8 5.5 %collective-permute-start.51 = (f32[3,1,4,64]{3,2,1,0:T(4,128)S(1)}, f32[3,1,4,64]{3,2,1,0:T(4,128)S(1)}, u32[]{:S(2)}, u32[]{:S(2)}) collective-permute-start(f32[3,1,4,64]{3,2,1,0:T(4,128)S(1)} %get-tuple-element.407), channel_id=1, source_target_pairs={{32,0},{64,32},{96,64},{128,96},{160,128},{192,160},{224,192},{33,... | collective-permute-start | bytes 9224 | tf_op jit(solution)/shard_map/ppermute | solution.py:19
  435.4 6.6 %collective-permute-start.52 = (f32[3,10,1,64]{3,2,1,0:T(1,128)S(1)}, f32[3,10,1,64]{3,2,1,0:T(1,128)S(1)}, u32[]{:S(2)}, u32[]{:S(2)}) collective-permute-start(f32[3,10,1,64]{3,2,1,0:T(1,128)S(1)} %get-tuple-element.392), channel_id=1, source_target_pairs={{0,1},{1,2},{2,3},{3,4},{4,5},{5,6},{6,7},{7,8},{8,9},{9,10},{10,1... | collective-permute-start | bytes 23048 | tf_op jit(solution)/shard_map/ppermute | solution.py:18
  437.3 8.9 %collective-permute-start.53 = (f32[3,10,1,64]{3,2,1,0:T(1,128)S(1)}, f32[3,10,1,64]{3,2,1,0:T(1,128)S(1)}, u32[]{:S(2)}, u32[]{:S(2)}) collective-permute-start(f32[3,10,1,64]{3,2,1,0:T(1,128)S(1)} %get-tuple-element.393), channel_id=1, source_target_pairs={{1,0},{2,1},{3,2},{4,3},{5,4},{6,5},{7,6},{8,7},{9,8},{10,9},{11,1... | collective-permute-start | bytes 23048 | tf_op jit(solution)/shard_map/ppermute | solution.py:19
Sparse Core Ops, SparseCore 0:
  32.9 134.5 all-gather.1
